TPU v7x, 32 devices: a whole 2x2x4 slice. The times are simulated.
32 devices in a mesh: groups: 2 (over y), slab: 4 (over z), batch: 2 (over x), chan: 2 (over core).
Axes of the slice: x: 2, y: 2, z: 4, core: 2. Of those that a mesh axis runs over, the one named last changes fastest.
Arguments:
- volume: bfloat16 [16, 8, 4, 8, 128], P(('groups', 'batch'), 'slab'), parts along dimension 0, may hold values from -6 to 6
- targets: float32 [16, 4], P(('groups', 'batch')), parts along dimension 0, may hold values from -1 to 1
- front_weight: bfloat16 [3, 3, 3, 128, 128], P(None, None, None, None, 'chan'), may hold values from -0.109375 to 0.109375
- stride_weight: bfloat16 [3, 3, 3, 128, 256], P(None, None, None, 'chan'), may hold values from -0.109375 to 0.109375
- hidden_weight: float32 [256, 128], P('chan'), may hold values from -0.375 to 0.375
- output_weight: float32 [128, 4], replicated, may hold values from -0.5 to 0.5
Outputs:
- grad_front: float32 [6, 3, 3, 128, 128], P('groups', None, None, None, 'chan'), parts along dimension 0
- grad_stride: float32 [6, 3, 3, 128, 256], P('groups', None, None, 'chan'), parts along dimension 0
- grad_hidden: float32 [512, 128], P(('groups', 'chan')), parts along dimension 0
- grad_output: float32 [256, 4], P('groups'), parts along dimension 0
- loss: float32 [2], P('groups'), parts along dimension 0
There are 2 independent parts, one for each index of `groups`. A program takes and returns all parts, laid end to end along the dimension named above; an argument that names none is the same for every part. Nothing has to cross between parts.
All inputs are finite; a program needn't handle non-finite values.
Results may differ from a plain program's by a relative error of at most 0.0052.
Values may be sent and summed in bfloat16 or wider, within the bound.
A program may use at most 64 MiB of HBM per device.

v0:
```python
import jax
import jax.numpy as jnp
from jax import lax
from jax.sharding import PartitionSpec as P


def with_halo(cells, sides, width):
    for axis, dim in sides:
        count = lax.axis_size(axis)
        ends = count - 1
        head = lax.slice_in_dim(cells, 0, width, axis=dim)
        tail = lax.slice_in_dim(cells, cells.shape[dim] - width, cells.shape[dim], axis=dim)
        cells = jnp.concatenate(
            [
                lax.ppermute(tail, axis, [(i, (i + 1) % count) for i in range(ends)]),
                cells,
                lax.ppermute(head, axis, [((i + 1) % count, i) for i in range(ends)]),
            ],
            axis=dim,
        )
    return cells


def swish_slope(preact):
    logistic = jax.nn.sigmoid(preact)
    return logistic * (1.0 + preact * (1.0 - logistic))


def tap_window(padded, tap_z, tap_x, tap_y, extent_z, extent_x, extent_y, stride):
    if stride == 1:
        return padded[
            :, tap_z : tap_z + extent_z, tap_x : tap_x + extent_x, tap_y : tap_y + extent_y, :
        ]
    leading = padded.shape[0]
    channels = padded.shape[-1]
    folded = padded.reshape(leading, extent_z + 1, 2, extent_x + 1, 2, extent_y + 1, 2, channels)
    return folded[
        :,
        tap_z // 2 : tap_z // 2 + extent_z,
        tap_z % 2,
        tap_x // 2 : tap_x // 2 + extent_x,
        tap_x % 2,
        tap_y // 2 : tap_y // 2 + extent_y,
        tap_y % 2,
        :,
    ]


def conv_apply(padded, weight, extent_z, extent_x, extent_y, stride):
    summed = None
    for tap_z in range(3):
        for tap_x in range(3):
            for tap_y in range(3):
                window = tap_window(
                    padded, tap_z, tap_x, tap_y, extent_z, extent_x, extent_y, stride
                )
                flat_tap = window.reshape(-1, window.shape[-1])
                contrib = jnp.dot(
                    flat_tap, weight[tap_z, tap_x, tap_y], preferred_element_type=jnp.float32
                )
                summed = contrib if summed is None else summed + contrib
    return summed.reshape(padded.shape[0], extent_z, extent_x, extent_y, weight.shape[-1])


def kernel_grad(padded, grad_out, extent_z, extent_x, extent_y, stride):
    flat_grad = grad_out.reshape(-1, grad_out.shape[-1])
    results = []
    for tap_z in range(3):
        for tap_x in range(3):
            for tap_y in range(3):
                window = tap_window(
                    padded, tap_z, tap_x, tap_y, extent_z, extent_x, extent_y, stride
                )
                flat_tap = window.reshape(-1, window.shape[-1])
                results.append(
                    lax.dot_general(
                        flat_tap,
                        flat_grad,
                        (((0,), (0,)), ((), ())),
                        preferred_element_type=jnp.float32,
                    )
                )
    return jnp.stack(results).reshape(3, 3, 3, padded.shape[-1], grad_out.shape[-1])


def input_grad(grad_out, weight, extent_z, extent_x, extent_y):
    leading = grad_out.shape[0]
    channels = weight.shape[3]
    flat_grad = grad_out.reshape(-1, grad_out.shape[-1])
    buckets = {}
    for tap_z in range(3):
        for tap_x in range(3):
            for tap_y in range(3):
                contrib = lax.dot_general(
                    flat_grad,
                    weight[tap_z, tap_x, tap_y],
                    (((1,), (1,)), ((), ())),
                    preferred_element_type=jnp.float32,
                )
                contrib = contrib.reshape(leading, extent_z, extent_x, extent_y, channels)
                placed = jnp.pad(
                    contrib,
                    (
                        (0, 0),
                        (tap_z // 2, 1 - tap_z // 2),
                        (tap_x // 2, 1 - tap_x // 2),
                        (tap_y // 2, 1 - tap_y // 2),
                        (0, 0),
                    ),
                )
                parity = (tap_z % 2, tap_x % 2, tap_y % 2)
                buckets[parity] = placed if parity not in buckets else buckets[parity] + placed
    planes_z = []
    for par_z in range(2):
        planes_x = []
        for par_x in range(2):
            planes_x.append(jnp.stack([buckets[par_z, par_x, par_y] for par_y in range(2)], axis=4))
        planes_z.append(jnp.stack(planes_x, axis=3))
    assembled = jnp.stack(planes_z, axis=2)
    assembled = assembled.reshape(
        leading, 2 * extent_z + 2, 2 * extent_x + 2, 2 * extent_y + 2, channels
    )
    return assembled[:, 1:-1, 1:-1, 1:-1, :]


def body(volume, targets, front_weight, stride_weight, hidden_weight, output_weight):
    highest = lax.Precision.HIGHEST
    slabs = lax.axis_size("slab")
    batches = lax.axis_size("batch")
    inner = front_weight.shape[-1]
    leading, thick, extent_x, extent_y, channels = volume.shape
    depth = thick * slabs
    outputs = output_weight.shape[-1]
    haloed = with_halo(volume, (("slab", 1),), 1)
    padded = jnp.pad(haloed, ((0, 0), (0, 0), (1, 1), (1, 1), (0, 0)))
    front_pre = conv_apply(padded, front_weight, thick, extent_x, extent_y, 1)
    front_act = jax.nn.silu(front_pre).astype(jnp.bfloat16)
    merged = front_act.reshape(leading, thick, extent_x, extent_y * inner)
    sample_act = lax.all_to_all(merged, "slab", split_axis=0, concat_axis=1, tiled=True)
    sample_act = sample_act.reshape(1, depth, extent_x, extent_y, inner)
    half_z = depth // 2
    half_x = extent_x // 2
    half_y = extent_y // 2
    cells = half_z * half_x * half_y
    stride_pad = jnp.pad(sample_act, ((0, 0), (1, 1), (1, 1), (1, 1), (0, 0)))
    partial_pre = conv_apply(stride_pad, stride_weight, half_z, half_x, half_y, 2)
    stride_pre = lax.psum_scatter(partial_pre, "chan", scatter_dimension=4, tiled=True)
    pooled = jnp.sum(jax.nn.silu(stride_pre), axis=(0, 1, 2, 3)) / cells
    hidden_pre = lax.psum(jnp.dot(pooled, hidden_weight, precision=highest), "chan")
    hidden_act = jax.nn.silu(hidden_pre)
    predicted = jnp.dot(hidden_act, output_weight, precision=highest)
    target_row = lax.dynamic_index_in_dim(targets, lax.axis_index("slab"), 0, keepdims=False)
    residual = predicted - target_row
    squared = jnp.sum(residual * residual)
    grad_output = jnp.outer(hidden_act, residual)
    grad_hidden_pre = jnp.dot(output_weight, residual, precision=highest) * swish_slope(hidden_pre)
    grad_hidden = jnp.outer(pooled, grad_hidden_pre)
    grad_pooled = jnp.dot(hidden_weight, grad_hidden_pre, precision=highest)
    grad_stride_pre = (grad_pooled / cells * swish_slope(stride_pre)).astype(jnp.bfloat16)
    full_grad = lax.all_gather(grad_stride_pre, "chan", axis=4, tiled=True)
    grad_stride = kernel_grad(stride_pad, full_grad, half_z, half_x, half_y, 2)
    grad_act = input_grad(full_grad, stride_weight, half_z, half_x, half_y).astype(jnp.bfloat16)
    returned = lax.all_to_all(
        grad_act.reshape(1, depth, extent_x, extent_y * inner),
        "slab",
        split_axis=1,
        concat_axis=0,
        tiled=True,
    )
    returned = returned.reshape(leading, thick, extent_x, extent_y, inner)
    grad_front_pre = (returned * swish_slope(front_pre)).astype(jnp.bfloat16)
    grad_front = kernel_grad(padded, grad_front_pre, thick, extent_x, extent_y, 1)
    grad_front, grad_stride, grad_hidden, grad_output, squared = lax.psum(
        (grad_front, grad_stride, grad_hidden, grad_output, squared), ("slab", "batch")
    )
    loss = (squared / (slabs * batches * outputs)).reshape(1)
    return (grad_front, grad_stride, grad_hidden, grad_output, loss)


def solution(mesh):
    in_specs = (
        P(("groups", "batch"), "slab", None, None, None),
        P(("groups", "batch"), None),
        P(None, None, None, None, "chan"),
        P(None, None, None, "chan", None),
        P("chan", None),
        P(),
    )
    out_specs = (
        P("groups", None, None, None, "chan"),
        P("groups", None, None, "chan", None),
        P(("groups", "chan"), None),
        P("groups", None),
        P("groups"),
    )
    return jax.shard_map(body, mesh=mesh, in_specs=in_specs, out_specs=out_specs, check_vma=False)
```

profile of v0, /device:TPU:0, one launch (start us, length us, event | category | flops | bytes accessed | tf_op | source)
XLA Modules:
  0.0 213.3 jit_solution(12655027647742667064)
XLA Ops:
  7.2 0.8 fusion.298
  8.0 4.9 %collective-permute-start = (bf16[4,1,4,8,128]{4,3,2,1,0:T(8,128)(2,1)S(1)}, bf16[4,1,4,8,128]{4,3,2,1,0:T(8,128)(2,1)S(1)}, u32[]{:S(2)}, u32[]{:S(2)}) collective-permute-start(bf16[4,1,4,8,128]{4,3,2,1,0:T(8,128)(2,1)S(1)} %get-tuple-element.63), channel_id=1, source_target_pairs={{0,4},{4,8},{8,12},{1,5},{5,9},{9,13},{2,6},{6,10},{10,14},{3,7},{... | collective-permute-start | bytes 98312 | tf_op jit(solution)/shard_map/ppermute | solution.py:15
  13.0 1.4 collective-permute-start.1
  14.5 4.4 %collective-permute-done.1 = bf16[4,1,4,8,128]{4,3,2,1,0:T(8,128)(2,1)S(1)} collective-permute-done((bf16[4,1,4,8,128]{4,3,2,1,0:T(8,128)(2,1)S(1)}, bf16[4,1,4,8,128]{4,3,2,1,0:T(8,128)(2,1)S(1)}, u32[]{:S(2)}, u32[]{:S(2)}) %collective-permute-start.1) | collective-permute-done | bytes 32800 | tf_op jit(solution)/shard_map/ppermute | solution.py:17
  18.9 1.0 select_maximum_fusion
  19.9 0.2 fusion.294
  20.2 0.6 copy-done.6
  25.4 9.3 %all_to_all.8 = bf16[4,2,4,512]{3,2,1,0:T(4,128)(2,1)S(1)} all-to-all(bf16[4,2,4,512]{3,2,1,0:T(4,128)(2,1)S(1)} %fusion.65), channel_id=1, replica_groups=mesh['groups'=2,'slab'=4,'batch'=2,'chan'=2] {'slab'}, dimensions={0} | all-to-all | bytes 65536 | tf_op jit(solution)/shard_map/all_to_all | solution.py:139
  35.1 0.2 fusion.296
  39.2 0.8 copy.165
  40.0 1.9 reshape.469
  41.9 6.1 %reduce-scatter.4.cloned.1.call-done = f32[128,32]{1,0:T(8,128)} async-done(((f32[256,32]{1,0:T(8,128)}), f32[128,32]{1,0:T(8,128)}) %reduce-scatter.4.cloned.1.call-update) | async-done | bytes 16400
  48.0 1.5 reshape.470
  49.5 0.4 copy.166
  50.1 2.5 %psum.42 = f32[128]{0:T(128)S(1)} all-reduce(f32[128]{0:T(128)S(1)} %convolution_bitcast_fusion.83), channel_id=1, replica_groups=mesh['groups'=2,'slab'=4,'batch'=2,'chan'=2] {'chan'}, use_global_device_ids=true, to_apply=%region_2.3 | all-reduce | flops 128 | bytes 1024 | tf_op jit(solution)/shard_map/psum | solution.py:149
  52.6 1.4 multiply_reduce_fusion.1
  54.4 1.8 all_gather.3
  65.4 0.7 reshape.468
  66.1 4.8 %all-to-all-start.1 = ((bf16[1,8,4,512]{3,2,0,1:T(4,128)(2,1)}), bf16[1,8,4,512]{3,2,0,1:T(4,128)(2,1)S(1)}, u32[]{:S(2)}, u32[]{:S(2)}) async-start(bf16[1,8,4,512]{3,2,0,1:T(4,128)(2,1)} %reshape.468), calls=%async_computation.1 | async-start | bytes 65536 | tf_op jit(solution)/shard_map/all_to_all | solution.py:163
  71.0 0.7 broadcast_multiply_fusion
  71.7 4.9 %all-to-all-done.1 = bf16[1,8,4,512]{3,2,0,1:T(4,128)(2,1)S(1)} async-done(((bf16[1,8,4,512]{3,2,0,1:T(4,128)(2,1)}), bf16[1,8,4,512]{3,2,0,1:T(4,128)(2,1)S(1)}, u32[]{:S(2)}, u32[]{:S(2)}) %all-to-all-start.1) | async-done | bytes 32800 | tf_op jit(solution)/shard_map/all_to_all | solution.py:163
  76.8 0.2 fusion.54
  77.0 0.2 fusion.53
  77.2 0.2 fusion.52
  77.4 0.2 fusion.51
  77.8 0.2 fusion.50
  78.0 0.2 fusion.49
  78.2 0.2 fusion.48
  78.5 0.2 fusion.47
  78.7 0.2 fusion.46
  78.9 0.2 fusion.45
  79.1 0.2 fusion.44
  79.3 0.2 fusion.43
  79.5 0.2 fusion.42
  79.7 0.2 fusion.41
  79.9 0.2 fusion.40
  80.5 0.2 fusion.37
  81.1 0.2 fusion.34
  81.5 0.2 fusion.33
  81.7 0.2 fusion.32
  81.9 0.2 fusion.31
  82.1 0.2 fusion.30
  82.4 0.9 copy-done.5
  83.4 20.3 %all-reduce.29 = (f32[128,4]{0,1:T(4,128)}, f32[]{:T(128)}) all-reduce(f32[128,4]{0,1:T(4,128)S(1)} %broadcast_multiply_fusion.1, f32[]{:T(128)} %get-tuple-element.65), channel_id=1, replica_groups=mesh['groups'=2,'slab'=4,'batch'=2,'chan'=2] {'slab','batch'}, use_global_device_ids=true, to_apply=%region_6.7 | all-reduce | flops 513 | bytes 4104 | tf_op jit(solution)/shard_map/psum | solution.py:173
  104.3 96.9 %all-reduce.33.cloned.1.call-done = (f32[3,3,3,128,64]{3,4,2,1,0:T(8,128)}, f32[3,3,3,64,256]{4,3,2,1,0:T(8,128)}, f32[128,128]{1,0:T(8,128)}) async-done(((f32[3,3,3,128,64]{3,4,2,1,0:T(8,128)}, f32[3,3,3,64,256]{4,3,2,1,0:T(8,128)}, f32[128,128]{1,0:T(8,128)}), (f32[3,3,3,128,64]{3,4,2,1,0:T(8,128)}, f32[3,3,3,64,256]{4,3,2,1,0:T(8,128)}, f32[128,128]{1,0:T(8,128)})) %all-reduce.33.cloned.1.call-update) | async-done | bytes 2719760 | tf_op jit(solution)/shard_map/psum | solution.py:173
  201.2 2.3 %copy.225 = f32[3,3,3,128,64]{3,4,2,1,0:T(8,128)} copy(f32[3,3,3,128,64]{3,4,2,1,0:T(8,128)} %get-tuple-element.73) | data formatting | bytes 1769472
  203.5 1.2 copy.226
  204.7 0.6 copy.227
  (204 shorter events, 19.8 us)
Async XLA Ops:
  7.2 42.8 %copy-start = (f32[128,128]{1,0:T(8,128)S(1)}, f32[128,128]{1,0:T(8,128)}, u32[]{:S(2)}) copy-start(f32[128,128]{1,0:T(8,128)} %param.10) | copy-start | bytes 196612
  7.2 40.8 %reduce-scatter.4.cloned.1.call-start = ((), (), s32[]{:S(2)}) async-start(), calls=%async_computation.3 | async-start | bytes 196608
  8.0 6.5 %collective-permute-start = (bf16[4,1,4,8,128]{4,3,2,1,0:T(8,128)(2,1)S(1)}, bf16[4,1,4,8,128]{4,3,2,1,0:T(8,128)(2,1)S(1)}, u32[]{:S(2)}, u32[]{:S(2)}) collective-permute-start(bf16[4,1,4,8,128]{4,3,2,1,0:T(8,128)(2,1)S(1)} %get-tuple-element.63), channel_id=1, source_target_pairs={{0,4},{4,8},{8,12},{1,5},{5,9},{9,13},{2,6},{6,10},{10,14},{3,7},{... | collective-permute-start | bytes 98312 | tf_op jit(solution)/shard_map/ppermute | solution.py:15
  12.9 7.2 %copy-start.4 = (bf16[4,2,4,8,128]{4,3,2,1,0:T(8,128)(2,1)S(1)}, bf16[4,2,4,8,128]{4,3,2,1,0:T(8,128)(2,1)}, u32[]{:S(2)}) copy-start(bf16[4,2,4,8,128]{4,3,2,1,0:T(8,128)(2,1)} %param.6) | copy-start | bytes 196612
  13.0 5.9 %collective-permute-start.1 = (bf16[4,1,4,8,128]{4,3,2,1,0:T(8,128)(2,1)S(1)}, bf16[4,1,4,8,128]{4,3,2,1,0:T(8,128)(2,1)S(1)}, u32[]{:S(2)}, u32[]{:S(2)}) collective-permute-start(bf16[4,1,4,8,128]{4,3,2,1,0:T(8,128)(2,1)S(1)} %get-tuple-element.64), channel_id=1, source_target_pairs={{4,0},{8,4},{12,8},{5,1},{9,5},{13,9},{6,2},{10,6},{14,10},{7,3},{... | collective-permute-start | bytes 98312 | tf_op jit(solution)/shard_map/ppermute | solution.py:17
  19.9 1.0 copy-start.6
  24.8 10.9 %copy-start.1 = (bf16[3,3,3,64,256]{4,3,2,1,0:T(8,128)(2,1)S(1)}, bf16[3,3,3,64,256]{4,3,2,1,0:T(8,128)(2,1)}, u32[]{:S(2)}) copy-start(bf16[3,3,3,64,256]{4,3,2,1,0:T(8,128)(2,1)} %param.9) | copy-start | bytes 2654212
  39.2 13.4 %copy-start.8 = (f32[128,4]{0,1:T(4,128)S(1)}, f32[128,4]{0,1:T(4,128)}, u32[]{:S(2)}) copy-start(f32[128,4]{0,1:T(4,128)} %param.11) | copy-start | bytes 6148
  64.7 12.0 %copy-start.2 = (f32[27,64,256]{2,1,0:T(8,128)}, f32[27,64,256]{2,1,0:T(8,128)S(1)}, u32[]{:S(2)}) copy-start(f32[27,64,256]{2,1,0:T(8,128)S(1)} %fusion) | copy-start | bytes 5308420
  66.1 10.5 %all-to-all-start.1 = ((bf16[1,8,4,512]{3,2,0,1:T(4,128)(2,1)}), bf16[1,8,4,512]{3,2,0,1:T(4,128)(2,1)S(1)}, u32[]{:S(2)}, u32[]{:S(2)}) async-start(bf16[1,8,4,512]{3,2,0,1:T(4,128)(2,1)} %reshape.468), calls=%async_computation.1 | async-start | bytes 65536 | tf_op jit(solution)/shard_map/all_to_all | solution.py:163
  71.0 130.2 %all-reduce.33.cloned.1.call-start = ((), (), s32[]{:S(2)}) async-start(), calls=%async_computation.4 | async-start | bytes 5439488 | tf_op jit(solution)/shard_map/psum | solution.py:173
  82.4 0.9 copy-start.5
  201.2 2.3 %copy-start.3 = (f32[3,3,3,64,256]{4,3,2,1,0:T(8,128)S(1)}, f32[3,3,3,64,256]{4,3,2,1,0:T(8,128)}, u32[]{:S(2)}) copy-start(f32[3,3,3,64,256]{4,3,2,1,0:T(8,128)} %get-tuple-element.74) | copy-start | bytes 5308420
  203.5 1.2 copy-start.7
Sparse Core Ops, SparseCore 0:
  42.0 5.8 reduce-scatter.3
  83.4 117.7 all-reduce.32
where the time goes:
time: 214 us; the launch traced here: 213 us
  waiting for transfers between devices  112 us (52%)
  blocking collectives  33.9 us (16%)
  matrix products  23.2 us (11%)
  between operations  16.7 us (8%)
  local copies, waits for them, and re-layouts  13.5 us (6%)
  starting transfers between devices  11.2 us (5%)
  other arithmetic  2.34 us (1%)
    psum x1, waiting for transfers between devices, body(): lax.psum((grad_front, grad_stride, grad_hidden, grad_output, squared), ('...  96.9 us
    psum x1, blocking collectives, body(): lax.psum((grad_front, grad_stride, grad_hidden, grad_output, squared), ('...  20.3 us
    unnamed x27, local copies, waits for them, and re-layouts  10.4 us
    dot_general x54, matrix products, kernel_grad(): lax.dot_general(flat_tap, flat_grad, (((0,), (0,)), ((), ())), preferred_...  10.2 us
    all_to_all x1, blocking collectives, body(): lax.all_to_all(merged, 'slab', split_axis=0, concat_axis=1, tiled=True)  9.32 us
    dot_general x54, matrix products, conv_apply(): jnp.dot(flat_tap, weight[tap_z, tap_x, tap_y], preferred_element_type=jnp...  7.54 us
    unnamed x3, waiting for transfers between devices  6.09 us
    all_to_all x1, waiting for transfers between devices, body(): lax.all_to_all(grad_act.reshape(1, depth, extent_x, extent_y * inner), 's...  4.94 us
  transfers between devices with their start and end apart: 5, of which 5 were waited for; matrix products, arithmetic and copies ran while one was open for 0% of the time, Pallas kernels for 0%

commit v1 on v0

--- a/solution.py
+++ b/solution.py
@@ -160,12 +160,20 @@
     full_grad = lax.all_gather(grad_stride_pre, "chan", axis=4, tiled=True)
     grad_stride = kernel_grad(stride_pad, full_grad, half_z, half_x, half_y, 2)
     grad_act = input_grad(full_grad, stride_weight, half_z, half_x, half_y).astype(jnp.bfloat16)
-    returned = lax.all_to_all(
-        grad_act.reshape(1, depth, extent_x, extent_y * inner),
-        "slab",
-        split_axis=1,
-        concat_axis=0,
-        tiled=True,
+    returned = jnp.concatenate(
+        lax.all_to_all(
+            jnp.stack(
+                jnp.split(
+                    grad_act.reshape(1, depth, extent_x, extent_y * inner),
+                    lax.axis_size("slab"),
+                    axis=1,
+                )
+            ),
+            "slab",
+            0,
+            0,
+        ),
+        axis=0,
     )
     returned = returned.reshape(leading, thick, extent_x, extent_y, inner)
     grad_front_pre = (returned * swish_slope(front_pre)).astype(jnp.bfloat16)

time: 214 us -> 214 us (level)
  no operation moved by 1% of the time
where the time goes in v1:
time: 214 us; the launch traced here: 213 us
  waiting for transfers between devices  112 us (52%)
  blocking collectives  33.9 us (16%)
  matrix products  23.2 us (11%)
  between operations  16.7 us (8%)
  local copies, waits for them, and re-layouts  13 us (6%)
  starting transfers between devices  11.2 us (5%)
  other arithmetic  3.01 us (1%)
    psum x1, waiting for transfers between devices, body(): lax.psum((grad_front, grad_stride, grad_hidden, grad_output, squared), ('...  96.9 us
    psum x1, blocking collectives, body(): lax.psum((grad_front, grad_stride, grad_hidden, grad_output, squared), ('...  20.3 us
    unnamed x27, local copies, waits for them, and re-layouts  10.4 us
    dot_general x54, matrix products, kernel_grad(): lax.dot_general(flat_tap, flat_grad, (((0,), (0,)), ((), ())), preferred_...  10.2 us
    all_to_all x1, blocking collectives, body(): lax.all_to_all(merged, 'slab', split_axis=0, concat_axis=1, tiled=True)  9.32 us
    dot_general x54, matrix products, conv_apply(): jnp.dot(flat_tap, weight[tap_z, tap_x, tap_y], preferred_element_type=jnp...  7.54 us
    unnamed x3, waiting for transfers between devices  6.09 us
    all_to_all x1, waiting for transfers between devices, body(): lax.all_to_all(jnp.stack(jnp.split(grad_act.reshape(1, depth, extent_x, e...  4.94 us
  transfers between devices with their start and end apart: 5, of which 5 were waited for; matrix products, arithmetic and copies ran while one was open for 0% of the time, Pallas kernels for 0%

profile of v1, /device:TPU:0, one launch (start us, length us, event | category | flops | bytes accessed | tf_op | source)
XLA Modules:
  0.0 213.4 jit_solution(3112192125102113100)
XLA Ops:
  7.2 0.8 fusion.299
  8.0 4.9 %collective-permute-start = (bf16[4,1,4,8,128]{4,3,2,1,0:T(8,128)(2,1)S(1)}, bf16[4,1,4,8,128]{4,3,2,1,0:T(8,128)(2,1)S(1)}, u32[]{:S(2)}, u32[]{:S(2)}) collective-permute-start(bf16[4,1,4,8,128]{4,3,2,1,0:T(8,128)(2,1)S(1)} %get-tuple-element.63), channel_id=1, source_target_pairs={{0,4},{4,8},{8,12},{1,5},{5,9},{9,13},{2,6},{6,10},{10,14},{3,7},{... | collective-permute-start | bytes 98312 | tf_op jit(solution)/shard_map/ppermute | solution.py:15
  13.0 1.4 collective-permute-start.1
  14.5 4.4 %collective-permute-done.1 = bf16[4,1,4,8,128]{4,3,2,1,0:T(8,128)(2,1)S(1)} collective-permute-done((bf16[4,1,4,8,128]{4,3,2,1,0:T(8,128)(2,1)S(1)}, bf16[4,1,4,8,128]{4,3,2,1,0:T(8,128)(2,1)S(1)}, u32[]{:S(2)}, u32[]{:S(2)}) %collective-permute-start.1) | collective-permute-done | bytes 32800 | tf_op jit(solution)/shard_map/ppermute | solution.py:17
  18.9 1.0 select_maximum_fusion
  19.9 0.2 fusion.295
  20.2 0.6 copy-done.6
  25.4 9.3 %all_to_all.14 = bf16[4,2,4,512]{3,2,1,0:T(4,128)(2,1)S(1)} all-to-all(bf16[4,2,4,512]{3,2,1,0:T(4,128)(2,1)S(1)} %fusion.66), channel_id=1, replica_groups=mesh['groups'=2,'slab'=4,'batch'=2,'chan'=2] {'slab'}, dimensions={0} | all-to-all | bytes 65536 | tf_op jit(solution)/shard_map/all_to_all | solution.py:139
  35.1 0.2 fusion.297
  39.2 0.8 copy.170
  40.0 1.9 reshape.463
  41.9 6.1 %reduce-scatter.4.cloned.1.call-done = f32[128,32]{1,0:T(8,128)} async-done(((f32[256,32]{1,0:T(8,128)}), f32[128,32]{1,0:T(8,128)}) %reduce-scatter.4.cloned.1.call-update) | async-done | bytes 16400
  48.0 1.5 reshape.464
  49.5 0.4 copy.171
  50.1 2.5 %psum.42 = f32[128]{0:T(128)S(1)} all-reduce(f32[128]{0:T(128)S(1)} %convolution_bitcast_fusion.83), channel_id=1, replica_groups=mesh['groups'=2,'slab'=4,'batch'=2,'chan'=2] {'chan'}, use_global_device_ids=true, to_apply=%region_2.3 | all-reduce | flops 128 | bytes 1024 | tf_op jit(solution)/shard_map/psum | solution.py:149
  52.6 1.4 multiply_reduce_fusion.1
  54.4 1.8 all_gather.3
  65.6 0.7 pad_maximum_fusion.1
  66.3 4.8 %all-to-all-start.1 = ((bf16[4,1,2,4,512]{4,2,3,1,0:T(2,128)(2,1)}), bf16[4,1,2,4,512]{4,2,3,1,0:T(2,128)(2,1)S(1)}, u32[]{:S(2)}, u32[]{:S(2)}) async-start(bf16[4,1,2,4,512]{4,2,3,1,0:T(2,128)(2,1)} %pad_maximum_fusion.1), calls=%async_computation.1 | async-start | bytes 65536 | tf_op jit(solution)/shard_map/all_to_all | solution.py:164
  71.1 0.7 broadcast_multiply_fusion
  71.8 4.9 %all-to-all-done.1 = bf16[4,1,2,4,512]{4,2,3,1,0:T(2,128)(2,1)S(1)} async-done(((bf16[4,1,2,4,512]{4,2,3,1,0:T(2,128)(2,1)}), bf16[4,1,2,4,512]{4,2,3,1,0:T(2,128)(2,1)S(1)}, u32[]{:S(2)}, u32[]{:S(2)}) %all-to-all-start.1) | async-done | bytes 32800 | tf_op jit(solution)/shard_map/all_to_all | solution.py:164
  76.9 0.2 fusion.54
  77.3 0.2 fusion.52
  77.5 0.2 fusion.51
  77.9 0.2 fusion.50
  78.1 0.2 fusion.49
  78.3 0.2 fusion.48
  78.6 0.2 fusion.47
  78.8 0.2 fusion.46
  79.0 0.2 fusion.45
  79.2 0.2 fusion.44
  79.4 0.2 fusion.43
  79.6 0.2 fusion.42
  79.8 0.2 fusion.41
  80.0 0.2 fusion.40
  80.6 0.2 fusion.37
  80.8 0.2 fusion.36
  81.2 0.2 fusion.34
  81.6 0.2 fusion.33
  81.8 0.2 fusion.32
  82.0 0.2 fusion.31
  82.2 0.2 fusion.30
  82.5 0.9 copy-done.5
  83.5 20.3 %all-reduce.29 = (f32[128,4]{0,1:T(4,128)}, f32[]{:T(128)}) all-reduce(f32[128,4]{0,1:T(4,128)S(1)} %broadcast_multiply_fusion.1, f32[]{:T(128)} %get-tuple-element.69), channel_id=1, replica_groups=mesh['groups'=2,'slab'=4,'batch'=2,'chan'=2] {'slab','batch'}, use_global_device_ids=true, to_apply=%region_6.7 | all-reduce | flops 513 | bytes 4104 | tf_op jit(solution)/shard_map/psum | solution.py:181
  104.4 96.9 %all-reduce.33.cloned.1.call-done = (f32[3,3,3,128,64]{3,4,2,1,0:T(8,128)}, f32[3,3,3,64,256]{4,3,2,1,0:T(8,128)}, f32[128,128]{1,0:T(8,128)}) async-done(((f32[3,3,3,128,64]{3,4,2,1,0:T(8,128)}, f32[3,3,3,64,256]{4,3,2,1,0:T(8,128)}, f32[128,128]{1,0:T(8,128)}), (f32[3,3,3,128,64]{3,4,2,1,0:T(8,128)}, f32[3,3,3,64,256]{4,3,2,1,0:T(8,128)}, f32[128,128]{1,0:T(8,128)})) %all-reduce.33.cloned.1.call-update) | async-done | bytes 2719760 | tf_op jit(solution)/shard_map/psum | solution.py:181
  201.3 2.3 %copy.232 = f32[3,3,3,128,64]{3,4,2,1,0:T(8,128)} copy(f32[3,3,3,128,64]{3,4,2,1,0:T(8,128)} %get-tuple-element.77) | data formatting | bytes 1769472
  203.6 1.2 copy.233
  204.8 0.6 copy.234
  (206 shorter events, 19.9 us)
Async XLA Ops:
  7.2 42.8 %copy-start = (f32[128,128]{1,0:T(8,128)S(1)}, f32[128,128]{1,0:T(8,128)}, u32[]{:S(2)}) copy-start(f32[128,128]{1,0:T(8,128)} %param.10) | copy-start | bytes 196612
  7.2 40.8 %reduce-scatter.4.cloned.1.call-start = ((), (), s32[]{:S(2)}) async-start(), calls=%async_computation.3 | async-start | bytes 196608
  8.0 6.5 %collective-permute-start = (bf16[4,1,4,8,128]{4,3,2,1,0:T(8,128)(2,1)S(1)}, bf16[4,1,4,8,128]{4,3,2,1,0:T(8,128)(2,1)S(1)}, u32[]{:S(2)}, u32[]{:S(2)}) collective-permute-start(bf16[4,1,4,8,128]{4,3,2,1,0:T(8,128)(2,1)S(1)} %get-tuple-element.63), channel_id=1, source_target_pairs={{0,4},{4,8},{8,12},{1,5},{5,9},{9,13},{2,6},{6,10},{10,14},{3,7},{... | collective-permute-start | bytes 98312 | tf_op jit(solution)/shard_map/ppermute | solution.py:15
  12.9 7.2 %copy-start.4 = (bf16[4,2,4,8,128]{4,3,2,1,0:T(8,128)(2,1)S(1)}, bf16[4,2,4,8,128]{4,3,2,1,0:T(8,128)(2,1)}, u32[]{:S(2)}) copy-start(bf16[4,2,4,8,128]{4,3,2,1,0:T(8,128)(2,1)} %param.6) | copy-start | bytes 196612
  13.0 5.9 %collective-permute-start.1 = (bf16[4,1,4,8,128]{4,3,2,1,0:T(8,128)(2,1)S(1)}, bf16[4,1,4,8,128]{4,3,2,1,0:T(8,128)(2,1)S(1)}, u32[]{:S(2)}, u32[]{:S(2)}) collective-permute-start(bf16[4,1,4,8,128]{4,3,2,1,0:T(8,128)(2,1)S(1)} %get-tuple-element.64), channel_id=1, source_target_pairs={{4,0},{8,4},{12,8},{5,1},{9,5},{13,9},{6,2},{10,6},{14,10},{7,3},{... | collective-permute-start | bytes 98312 | tf_op jit(solution)/shard_map/ppermute | solution.py:17
  19.9 1.0 copy-start.6
  24.8 10.9 %copy-start.1 = (bf16[3,3,3,64,256]{4,3,2,1,0:T(8,128)(2,1)S(1)}, bf16[3,3,3,64,256]{4,3,2,1,0:T(8,128)(2,1)}, u32[]{:S(2)}) copy-start(bf16[3,3,3,64,256]{4,3,2,1,0:T(8,128)(2,1)} %param.9) | copy-start | bytes 2654212
  39.2 13.4 %copy-start.8 = (f32[128,4]{0,1:T(4,128)S(1)}, f32[128,4]{0,1:T(4,128)}, u32[]{:S(2)}) copy-start(f32[128,4]{0,1:T(4,128)} %param.11) | copy-start | bytes 6148
  64.7 7.1 %copy-start.2 = (f32[27,64,256]{2,1,0:T(8,128)}, f32[27,64,256]{2,1,0:T(8,128)S(1)}, u32[]{:S(2)}) copy-start(f32[27,64,256]{2,1,0:T(8,128)S(1)} %fusion) | copy-start | bytes 5308420
  66.3 10.5 %all-to-all-start.1 = ((bf16[4,1,2,4,512]{4,2,3,1,0:T(2,128)(2,1)}), bf16[4,1,2,4,512]{4,2,3,1,0:T(2,128)(2,1)S(1)}, u32[]{:S(2)}, u32[]{:S(2)}) async-start(bf16[4,1,2,4,512]{4,2,3,1,0:T(2,128)(2,1)} %pad_maximum_fusion.1), calls=%async_computation.1 | async-start | bytes 65536 | tf_op jit(solution)/shard_map/all_to_all | solution.py:164
  71.1 130.2 %all-reduce.33.cloned.1.call-start = ((), (), s32[]{:S(2)}) async-start(), calls=%async_computation.4 | async-start | bytes 5439488 | tf_op jit(solution)/shard_map/psum | solution.py:181
  82.4 0.9 copy-start.5
  201.3 2.3 %copy-start.3 = (f32[3,3,3,64,256]{4,3,2,1,0:T(8,128)S(1)}, f32[3,3,3,64,256]{4,3,2,1,0:T(8,128)}, u32[]{:S(2)}) copy-start(f32[3,3,3,64,256]{4,3,2,1,0:T(8,128)} %get-tuple-element.78) | copy-start | bytes 5308420
  203.6 1.2 copy-start.7
Sparse Core Ops, SparseCore 0:
  42.0 5.8 reduce-scatter.3
  83.5 117.7 all-reduce.32
